TPU v7x, 128 devices: a whole 4x4x4 slice. The times are simulated.
128 devices in a mesh: seq: 32 (over x_hi, z, y), dp: 4 (over x_lo, core).
Axes of the slice: x: 4 (x_hi: 2, x_lo: 2; x = x_hi * 2 + x_lo), y: 4, z: 4, core: 2. Of those that a mesh axis runs over, the one named last changes fastest.
Arguments:
- query_proj: bfloat16 [4, 2048, 4096], P('dp', None, 'seq'), may hold values from -6 to 6
- key_proj: bfloat16 [4, 2048, 4096], P('dp', None, 'seq'), may hold values from -6 to 6
- value_proj: bfloat16 [4, 2048, 4096], P('dp', None, 'seq'), may hold values from -6 to 6
- grad_out: bfloat16 [4, 2048, 4096], P('dp', None, 'seq'), may hold values from -6 to 6
- mode_gain: float32 [2048, 16], P('seq'), may hold values from -3 to 3
- decay_rate: float32 [2048, 16], P('seq'), may hold values from 0.5 to 128
- skip_gain: float32 [2048], P('seq'), may hold values from -4 to 4
Outputs:
- grad_query: bfloat16 [4, 2048, 4096], P('dp', None, 'seq')
- grad_key: bfloat16 [4, 2048, 4096], P('dp', None, 'seq')
- grad_value: bfloat16 [4, 2048, 4096], P('dp', None, 'seq')
- grad_modes: float32 [2048, 16], P('seq')
- grad_rate: float32 [2048, 16], P('seq')
- grad_skip: float32 [2048], P('seq')
All inputs are finite; a program needn't handle non-finite values.
Results may differ from a plain program's by a relative error of at most 0.0095.
Values may be sent and summed in bfloat16 or wider, within the bound.
No kernel may reach another device: no remote copies, remote signals or barrier semaphores. Data moves between devices by JAX's collectives and lax.ppermute only.
A program may use at most 128 MiB of HBM per device.

v0:
```python
import math

import jax
import jax.numpy as jnp
from jax import lax
from jax.sharding import PartitionSpec as P

HIGHEST = lax.Precision.HIGHEST


def phase_table(left, right, modulus):
    wrapped = left[:, None] * right[None, :] % modulus
    angles = 2.0 * math.pi / modulus * wrapped.astype(jnp.float32)
    return (jnp.cos(angles), jnp.sin(angles))


def forward_dft(sig_re, sig_im, half_rows):
    channels = sig_re.shape[0]
    rows = 2 * half_rows
    columns = 2 * sig_re.shape[1] // rows
    padded_len = rows * columns
    shaped_re = sig_re.reshape(channels, half_rows, columns)
    shaped_im = sig_im.reshape(channels, half_rows, columns)
    row_index = jnp.arange(rows, dtype=jnp.int32)
    half_index = jnp.arange(half_rows, dtype=jnp.int32)
    col_index = jnp.arange(columns, dtype=jnp.int32)
    cos_one, sin_one = phase_table(row_index, half_index, rows)
    first_re = jnp.einsum("kt,ctj->ckj", cos_one, shaped_re, precision=HIGHEST) + jnp.einsum(
        "kt,ctj->ckj", sin_one, shaped_im, precision=HIGHEST
    )
    first_im = jnp.einsum("kt,ctj->ckj", cos_one, shaped_im, precision=HIGHEST) - jnp.einsum(
        "kt,ctj->ckj", sin_one, shaped_re, precision=HIGHEST
    )
    twist_cos, twist_sin = phase_table(row_index, col_index, padded_len)
    middle_re = first_re * twist_cos + first_im * twist_sin
    middle_im = first_im * twist_cos - first_re * twist_sin
    cos_two, sin_two = phase_table(col_index, col_index, columns)
    out_re = jnp.einsum("ckj,jm->ckm", middle_re, cos_two, precision=HIGHEST) + jnp.einsum(
        "ckj,jm->ckm", middle_im, sin_two, precision=HIGHEST
    )
    out_im = jnp.einsum("ckj,jm->ckm", middle_im, cos_two, precision=HIGHEST) - jnp.einsum(
        "ckj,jm->ckm", middle_re, sin_two, precision=HIGHEST
    )
    return (out_re, out_im)


def negate_freq(spec):
    turned = jnp.roll(jnp.flip(spec, 1), 1, axis=1)
    flipped = jnp.flip(turned, 2)
    first_row = (jnp.arange(spec.shape[1], dtype=jnp.int32) == 0)[None, :, None]
    return jnp.where(first_row, jnp.roll(flipped, 1, axis=2), flipped)


def split_pair(spec_re, spec_im):
    other_re = negate_freq(spec_re)
    other_im = negate_freq(spec_im)
    first = ((spec_re + other_re) * 0.5, (spec_im - other_im) * 0.5)
    second = ((spec_im + other_im) * 0.5, (other_re - spec_re) * 0.5)
    return (first, second)


def inverse_dft(spec_re, spec_im, half_rows):
    channels, rows, columns = spec_re.shape
    padded_len = rows * columns
    row_index = jnp.arange(rows, dtype=jnp.int32)
    half_index = jnp.arange(half_rows, dtype=jnp.int32)
    col_index = jnp.arange(columns, dtype=jnp.int32)
    cos_two, sin_two = phase_table(col_index, col_index, columns)
    back_re = jnp.einsum("ckm,mj->ckj", spec_re, cos_two, precision=HIGHEST) - jnp.einsum(
        "ckm,mj->ckj", spec_im, sin_two, precision=HIGHEST
    )
    back_im = jnp.einsum("ckm,mj->ckj", spec_im, cos_two, precision=HIGHEST) + jnp.einsum(
        "ckm,mj->ckj", spec_re, sin_two, precision=HIGHEST
    )
    twist_cos, twist_sin = phase_table(row_index, col_index, padded_len)
    middle_re = back_re * twist_cos - back_im * twist_sin
    middle_im = back_im * twist_cos + back_re * twist_sin
    cos_one, sin_one = phase_table(half_index, row_index, rows)
    out_re = jnp.einsum("tk,ckj->ctj", cos_one, middle_re, precision=HIGHEST) - jnp.einsum(
        "tk,ckj->ctj", sin_one, middle_im, precision=HIGHEST
    )
    out_im = jnp.einsum("tk,ckj->ctj", cos_one, middle_im, precision=HIGHEST) + jnp.einsum(
        "tk,ckj->ctj", sin_one, middle_re, precision=HIGHEST
    )
    out_len = half_rows * columns
    return (
        out_re.reshape(channels, out_len) / padded_len,
        out_im.reshape(channels, out_len) / padded_len,
    )


def channel_work(product, grad_mix, mode_gain, decay_rate, skip_gain):
    channels, length = product.shape
    half_rows = min(128, length // 2)
    half_ch = channels // 2
    positions = jnp.arange(length, dtype=jnp.float32) / length
    kernel = jnp.zeros((channels, length), jnp.float32)
    for which in range(mode_gain.shape[1]):
        kernel = kernel + mode_gain[:, which : which + 1] * jnp.exp(
            -decay_rate[:, which : which + 1] * positions[None, :]
        )
    kernel = kernel / math.sqrt(length)
    packed_re, packed_im = forward_dft(kernel[:half_ch], kernel[half_ch:], half_rows)
    low_kern, high_kern = split_pair(packed_re, packed_im)
    kern_re = jnp.concatenate([low_kern[0], high_kern[0]], axis=0)
    kern_im = jnp.concatenate([low_kern[1], high_kern[1]], axis=0)
    prod_f = product.astype(jnp.float32)
    gmix_f = grad_mix.astype(jnp.float32)
    joint_re, joint_im = forward_dft(prod_f, gmix_f, half_rows)
    prod_spec, gmix_spec = split_pair(joint_re, joint_im)
    prod_re, prod_im = prod_spec
    gmix_re, gmix_im = gmix_spec
    conv_re = kern_re * prod_re - kern_im * prod_im
    conv_im = kern_re * prod_im + kern_im * prod_re
    corr_re = kern_re * gmix_re + kern_im * gmix_im
    corr_im = kern_re * gmix_im - kern_im * gmix_re
    conv, corr = inverse_dft(conv_re - corr_im, conv_im + corr_re, half_rows)
    mixed = (conv + skip_gain[:, None] * prod_f).astype(jnp.bfloat16)
    grad_prod = (corr + skip_gain[:, None] * gmix_f).astype(jnp.bfloat16)
    lag_re = gmix_re * prod_re + gmix_im * prod_im
    lag_im = gmix_im * prod_re - gmix_re * prod_im
    lag_low, lag_high = inverse_dft(
        lag_re[:half_ch] - lag_im[half_ch:], lag_im[:half_ch] + lag_re[half_ch:], half_rows
    )
    lag_grad = jnp.concatenate([lag_low, lag_high], axis=0)
    mode_cols = []
    rate_cols = []
    for which in range(mode_gain.shape[1]):
        decay = jnp.exp(-decay_rate[:, which : which + 1] * positions[None, :])
        mode_cols.append(jnp.sum(lag_grad * decay, axis=1))
        rate_cols.append(
            -mode_gain[:, which] * jnp.sum(lag_grad * positions[None, :] * decay, axis=1)
        )
    mode_part = jnp.stack(mode_cols, axis=1)
    rate_part = jnp.stack(rate_cols, axis=1)
    skip_part = jnp.sum(gmix_f * prod_f, axis=1)
    return (mixed, grad_prod, (mode_part, rate_part, skip_part))


def body(query_proj, key_proj, value_proj, grad_out, mode_gain, decay_rate, skip_gain):
    moved = (
        lax.all_to_all(query_proj, "seq", split_axis=1, concat_axis=2, tiled=True),
        lax.all_to_all(key_proj, "seq", split_axis=1, concat_axis=2, tiled=True),
        lax.all_to_all(value_proj, "seq", split_axis=1, concat_axis=2, tiled=True),
        lax.all_to_all(grad_out, "seq", split_axis=1, concat_axis=2, tiled=True),
    )
    query_ch = moved[0][0].astype(jnp.float32)
    key_ch = moved[1][0].astype(jnp.float32)
    value_ch = moved[2][0].astype(jnp.float32)
    grad_ch = moved[3][0].astype(jnp.float32)
    product = (key_ch * value_ch).astype(jnp.bfloat16)
    grad_mix = (grad_ch * query_ch).astype(jnp.bfloat16)
    mixed, grad_prod, partial_sums = channel_work(
        product, grad_mix, mode_gain, decay_rate, skip_gain
    )
    query_grad = (grad_ch * mixed.astype(jnp.float32)).astype(jnp.bfloat16)
    key_grad = (grad_prod.astype(jnp.float32) * value_ch).astype(jnp.bfloat16)
    value_grad = (grad_prod.astype(jnp.float32) * key_ch).astype(jnp.bfloat16)
    returned = (
        lax.all_to_all(query_grad[None], "seq", split_axis=2, concat_axis=1, tiled=True),
        lax.all_to_all(key_grad[None], "seq", split_axis=2, concat_axis=1, tiled=True),
        lax.all_to_all(value_grad[None], "seq", split_axis=2, concat_axis=1, tiled=True),
    )
    grad_query = returned[0]
    grad_key = returned[1]
    grad_value = returned[2]
    totals = lax.psum((partial_sums[0], partial_sums[1], partial_sums[2]), "dp")
    length = mixed.shape[1]
    scale = 1.0 / math.sqrt(lax.axis_size("dp") * length)
    grad_modes = totals[0] * (scale / math.sqrt(length))
    grad_rate = totals[1] * (scale / math.sqrt(length))
    grad_skip = totals[2] * scale
    return (grad_query, grad_key, grad_value, grad_modes, grad_rate, grad_skip)


def solution(mesh):
    return jax.shard_map(
        body,
        mesh=mesh,
        in_specs=(
            P("dp", None, "seq"),
            P("dp", None, "seq"),
            P("dp", None, "seq"),
            P("dp", None, "seq"),
            P("seq", None),
            P("seq", None),
            P("seq"),
        ),
        out_specs=(
            P("dp", None, "seq"),
            P("dp", None, "seq"),
            P("dp", None, "seq"),
            P("seq", None),
            P("seq", None),
            P("seq"),
        ),
        check_vma=False,
    )
```

profile of v0, /device:TPU:1, one launch (start us, length us, event | category | flops | bytes accessed | tf_op | source)
XLA Modules:
  0.0 485.9 jit_solution(11262553688904226538)
XLA Ops:
  3.0 11.5 %reduce.1 = bf16[2048,128]{1,0:T(8,128)(2,1)S(1)} reduce(bf16[2048,1,128]{2,1,0:T(2,128)(2,1)S(1)} %bitcast.339, bf16[]{:T(256)} %broadcast.465), dimensions={1}, to_apply=%bitcast.304.reduce_sub_computation | reduce | bytes 1048578
  15.4 11.7 %all-to-all-start.1 = ((bf16[32,2,4096]{2,1,0:T(2,128)(2,1)}), bf16[32,2,4096]{2,1,0:T(2,128)(2,1)}, u32[]{:S(2)}, u32[]{:S(2)}) async-start(bf16[32,2,4096]{2,1,0:T(2,128)(2,1)} %reshape.354), calls=%async_computation.1 | async-start | bytes 1048576 | tf_op jit(solution)/shard_map/all_to_all | solution.py:143
  38.9 5.5 %fusion.55 = f32[32,32,256]{2,1,0:T(8,128)S(1)} fusion(f32[32,128,32]{2,1,0:T(8,128)} %reshape.335), kind=kOutput, calls=%fused_computation.186 | convolution fusion | flops 403111936 | bytes 1572864 | tf_op jit(solution)/shard_map/kt,ctj->ckj/dot_general | solution.py:31
  44.5 4.2 fusion.5
  67.9 8.9 %copy.216 = bf16[1,2048,128]{2,0,1:T(2,128)(2,1)} copy(bf16[1,2048,128]{2,1,0:T(8,128)(2,1)S(1)} %copy-done.32) | data formatting | bytes 1048576 | tf_op args[0]
  76.8 12.6 %reduce.3 = bf16[2048,128]{1,0:T(8,128)(2,1)S(1)} reduce(bf16[2048,1,128]{2,1,0:T(2,128)(2,1)} %bitcast.341, bf16[]{:T(256)} %broadcast.465), dimensions={1}, to_apply=%bitcast.302.reduce_sub_computation | reduce | bytes 1048578
  93.2 12.6 %reduce.4 = bf16[2048,128]{1,0:T(8,128)(2,1)S(1)} reduce(bf16[2048,1,128]{2,1,0:T(2,128)(2,1)} %bitcast.342, bf16[]{:T(256)} %broadcast.465), dimensions={1}, to_apply=%bitcast.303.reduce_sub_computation | reduce | bytes 1048578
  109.3 12.6 %reduce.2 = bf16[2048,128]{1,0:T(8,128)(2,1)S(1)} reduce(bf16[2048,1,128]{2,1,0:T(2,128)(2,1)} %bitcast.343, bf16[]{:T(256)} %broadcast.465), dimensions={1}, to_apply=%bitcast.305.reduce_sub_computation | reduce | bytes 1048578
  139.1 9.2 %all-to-all-start.2 = ((bf16[32,2,4096]{2,1,0:T(2,128)(2,1)}), bf16[32,2,4096]{2,1,0:T(2,128)(2,1)S(1)}, u32[]{:S(2)}, u32[]{:S(2)}) async-start(bf16[32,2,4096]{2,1,0:T(2,128)(2,1)} %reshape.356), calls=%async_computation.2 | async-start | bytes 1048576 | tf_op jit(solution)/shard_map/all_to_all | solution.py:144
  148.3 4.7 add_multiply_fusion.3
  159.0 6.9 %all-to-all-start.3 = ((bf16[32,2,4096]{2,1,0:T(2,128)(2,1)}), bf16[32,2,4096]{2,1,0:T(2,128)(2,1)S(1)}, u32[]{:S(2)}, u32[]{:S(2)}) async-start(bf16[32,2,4096]{2,1,0:T(2,128)(2,1)} %reshape.352), calls=%async_computation.3 | async-start | bytes 1048576 | tf_op jit(solution)/shard_map/all_to_all | solution.py:142
  167.7 9.1 %all-to-all-done.3 = bf16[32,2,4096]{2,1,0:T(2,128)(2,1)S(1)} async-done(((bf16[32,2,4096]{2,1,0:T(2,128)(2,1)}), bf16[32,2,4096]{2,1,0:T(2,128)(2,1)S(1)}, u32[]{:S(2)}, u32[]{:S(2)}) %all-to-all-start.3) | async-done | bytes 524320 | tf_op jit(solution)/shard_map/all_to_all | solution.py:142
  176.8 4.6 all-to-all-start
  184.1 8.0 %all-to-all-done = bf16[32,2,4096]{2,1,0:T(2,128)(2,1)} async-done(((bf16[32,2,4096]{2,1,0:T(2,128)(2,1)}), bf16[32,2,4096]{2,1,0:T(2,128)(2,1)}, u32[]{:S(2)}, u32[]{:S(2)}) %all-to-all-start) | async-done | bytes 524320 | tf_op jit(solution)/shard_map/all_to_all | solution.py:145
  214.2 4.2 reverse.17
  239.1 4.1 rev.23
  249.2 4.1 slice.285
  253.4 5.1 %multiply_subtract_fusion = (f32[64,256,32]{1,2,0:T(8,128)S(1)}, f32[64,256,32]{1,2,0:T(8,128)S(1)}, f32[64,256,32]{1,2,0:T(8,128)S(1)}, f32[64,256,32]{1,2,0:T(8,128)S(1)}, f32[64,256,32]{1,2,0:T(8,128)S(1)}) fusion(f32[64,256,32]{1,2,0:T(8,128)S(1)} %copy-done.4, f32[64,256,32]{1,2,0:T(8,128)} %rev.23, f32[64,256,31]{1,2,0:T(8,128)} %slice.291, ...), kind=kLoop, calls=%fused_computation.19 | loop fusion | flops 7864320 | bytes 23068928 | tf_op jit(solution)/shard_map/sub | solution.py:121
  308.3 5.2 %fusion.9 = f32[64,128,32]{1,2,0:T(8,128)} fusion(f32[64,32,128]{2,1,0:T(8,128)} %fusion.20, f32[64,256,32]{1,2,0:T(8,128)} %copy-done, f32[64,256,32]{1,2,0:T(8,128)S(1)} %convolution_subtract_fusion, f32[256,32]{0,1:T(8,128)S(1)} %get-tuple-element.138, f32[256,32]{0,1:T(8,128)S(1)} %get-tuple-element.139), kind=kOutput, calls=%fused_computation.56 | convolution fusion | flops 807862272 | bytes 6356992 | tf_op jit(solution)/shard_map/tk,ckj->ctj/dot_general | solution.py:82
  313.5 4.0 copy.155
  320.7 5.2 %fusion.7 = f32[64,128,32]{1,2,0:T(8,128)} fusion(f32[64,32,128]{2,1,0:T(8,128)} %fusion.19, f32[64,256,32]{1,2,0:T(8,128)S(1)} %convolution_subtract_fusion, f32[64,256,32]{1,2,0:T(8,128)} %copy-done, f32[256,32]{0,1:T(8,128)S(1)} %get-tuple-element.138, f32[256,32]{0,1:T(8,128)S(1)} %get-tuple-element.139), kind=kOutput, calls=%fused_computation.54 | convolution fusion | flops 807862272 | bytes 6356992 | tf_op jit(solution)/shard_map/tk,ckj->ctj/dot_general | solution.py:79
  330.7 6.0 %fusion.15 = (bf16[1,64,4096]{2,1,0:T(8,128)(2,1)S(1)}, bf16[1,64,4096]{2,1,0:T(8,128)(2,1)S(1)}, bf16[1,64,4096]{2,1,0:T(8,128)(2,1)}) fusion(f32[1,64,4096]{2,0,1:T(1,128)} %bitcast.332, f32[1,64,4096]{2,1,0:T(8,128)} %copy.159, f32[1,64,4096]{2,0,1:T(1,128)} %bitcast.331, f32[1,64,4096]{2,0,1:T(1,128)} %bitcast.333, f32[64]{0:T(128)S(1)} %copy-done.36, ...), kind=kLoop, calls=%fused_computation.66 | loop fusion | flops 4718592 | bytes 7864576 | tf_op jit(solution)/shard_map/convert_element_type | solution.py:158
  340.8 22.4 %reduce.7 = bf16[4096,64]{1,0:T(8,128)(2,1)S(1)} reduce(bf16[4096,1,64]{2,1,0:T(2,128)(2,1)S(1)} %bitcast.327, bf16[]{:T(256)} %broadcast.465), dimensions={1}, to_apply=%bitcast.284.reduce_sub_computation | reduce | bytes 1048578
  364.8 4.8 all-to-all-start.6
  369.7 5.7 %multiply_reduce_fusion.1 = (f32[64]{0:T(128)S(1)}, f32[64]{0:T(128)S(1)}, f32[64]{0:T(128)S(1)}, f32[64]{0:T(128)S(1)}, f32[64]{0:T(128)S(1)}, /*index=5*/f32[6...) fusion(f32[64]{0:T(128)S(1)} %get-tuple-element.134, ...), kind=kLoop, calls=%fused_computation.75 | loop fusion | flops 21231616 | bytes 1077248 | tf_op jit(solution)/shard_map/reduce_sum | solution.py:132
  378.2 22.4 %reduce.6 = bf16[4096,64]{1,0:T(8,128)(2,1)S(1)} reduce(bf16[4096,1,64]{2,1,0:T(2,128)(2,1)S(1)} %bitcast.328, bf16[]{:T(256)} %broadcast.465), dimensions={1}, to_apply=%bitcast.282.reduce_sub_computation | reduce | bytes 1048578
  402.2 9.9 %all-to-all-start.5 = ((bf16[32,2,4096]{2,1,0:T(2,128)(2,1)}), bf16[32,2,4096]{2,1,0:T(2,128)(2,1)}, u32[]{:S(2)}, u32[]{:S(2)}) async-start(bf16[32,2,4096]{2,1,0:T(2,128)(2,1)} %reshape.360), calls=%async_computation.5 | async-start | bytes 1048576 | tf_op jit(solution)/shard_map/all_to_all | solution.py:161
  415.6 22.4 %reduce.5 = bf16[4096,64]{1,0:T(8,128)(2,1)S(1)} reduce(bf16[4096,1,64]{2,1,0:T(2,128)(2,1)S(1)} %bitcast.324, bf16[]{:T(256)} %broadcast.465), dimensions={1}, to_apply=%bitcast.280.reduce_sub_computation | reduce | bytes 1048578
  439.7 14.1 %all-reduce = (f32[64,16]{0,1:T(8,128)S(1)}, f32[64,16]{0,1:T(8,128)S(1)}, f32[64]{0:T(128)S(1)}) all-reduce(f32[64,16]{0,1:T(8,128)S(1)} %stack.86, f32[64,16]{0,1:T(8,128)S(1)} %stack.87, f32[64]{0:T(128)S(1)} %multiply_reduce_fusion), channel_id=1, replica_groups=mesh['seq'=32,'dp'=4] {'dp'}, use_global_device_ids=true, to_apply=%region_16.17 | all-reduce | flops 2112 | bytes 16896 | tf_op jit(solution)/shard_map/psum | solution.py:167
  455.0 10.1 %all-to-all-start.4 = ((bf16[32,2,4096]{2,1,0:T(2,128)(2,1)}), bf16[32,2,4096]{2,1,0:T(2,128)(2,1)S(1)}, u32[]{:S(2)}, u32[]{:S(2)}) async-start(bf16[32,2,4096]{2,1,0:T(2,128)(2,1)} %reshape.358), calls=%async_computation.4 | async-start | bytes 1048576 | tf_op jit(solution)/shard_map/all_to_all | solution.py:160
  465.6 4.1 reshape.363
  473.2 4.1 reshape.361
  (213 shorter events, 203.7 us)
Async XLA Ops:
  2.4 24.8 %copy-start.35 = (f32[64,16]{0,1:T(8,128)S(1)}, f32[64,16]{0,1:T(8,128)}, u32[]{:S(2)}) copy-start(f32[64,16]{0,1:T(8,128)} %param.12) | copy-start | bytes 12292
  2.4 24.9 %copy-start.34 = (f32[64,16]{0,1:T(8,128)S(1)}, f32[64,16]{0,1:T(8,128)}, u32[]{:S(2)}) copy-start(f32[64,16]{0,1:T(8,128)} %param.11) | copy-start | bytes 12292
  15.4 123.6 %all-to-all-start.1 = ((bf16[32,2,4096]{2,1,0:T(2,128)(2,1)}), bf16[32,2,4096]{2,1,0:T(2,128)(2,1)}, u32[]{:S(2)}, u32[]{:S(2)}) async-start(bf16[32,2,4096]{2,1,0:T(2,128)(2,1)} %reshape.354), calls=%async_computation.1 | async-start | bytes 1048576 | tf_op jit(solution)/shard_map/all_to_all | solution.py:143
  32.1 6.8 %copy-start.6 = (f32[32,128,32]{2,1,0:T(8,128)}, f32[32,128,32]{2,1,0:T(8,128)S(1)}, u32[]{:S(2)}) copy-start(f32[32,128,32]{2,1,0:T(8,128)S(1)} %reshape.334) | copy-start | bytes 1572868
  38.9 5.5 %copy-start.8 = (f32[32,128,32]{2,1,0:T(8,128)S(1)}, f32[32,128,32]{2,1,0:T(8,128)}, u32[]{:S(2)}) copy-start(f32[32,128,32]{2,1,0:T(8,128)} %reshape.335) | copy-start | bytes 1572868
  44.5 4.2 copy-start.7
  54.9 4.5 copy-start.9
  66.5 66.7 %copy-start.18 = (f32[32,1,32]{1,2,0:T(8,128)}, f32[32,1,32]{1,2,0:T(8,128)S(1)}, u32[]{:S(2)}) copy-start(f32[32,1,32]{1,2,0:T(8,128)S(1)} %slice.298) | copy-start | bytes 12292
  136.8 11.5 %copy-start.10 = (f32[32,256,32]{1,2,0:T(8,128)S(1)}, f32[32,256,32]{1,2,0:T(8,128)}, u32[]{:S(2)}) copy-start(f32[32,256,32]{1,2,0:T(8,128)} %copy-done.9) | copy-start | bytes 3145732
  137.9 10.4 %copy-start.12 = (f32[32,256,32]{1,2,0:T(8,128)S(1)}, f32[32,256,32]{1,2,0:T(8,128)}, u32[]{:S(2)}) copy-start(f32[32,256,32]{1,2,0:T(8,128)} %copy-done.11) | copy-start | bytes 3145732
  139.1 19.9 %all-to-all-start.2 = ((bf16[32,2,4096]{2,1,0:T(2,128)(2,1)}), bf16[32,2,4096]{2,1,0:T(2,128)(2,1)S(1)}, u32[]{:S(2)}, u32[]{:S(2)}) async-start(bf16[32,2,4096]{2,1,0:T(2,128)(2,1)} %reshape.356), calls=%async_computation.2 | async-start | bytes 1048576 | tf_op jit(solution)/shard_map/all_to_all | solution.py:144
  159.0 17.8 %all-to-all-start.3 = ((bf16[32,2,4096]{2,1,0:T(2,128)(2,1)}), bf16[32,2,4096]{2,1,0:T(2,128)(2,1)S(1)}, u32[]{:S(2)}, u32[]{:S(2)}) async-start(bf16[32,2,4096]{2,1,0:T(2,128)(2,1)} %reshape.352), calls=%async_computation.3 | async-start | bytes 1048576 | tf_op jit(solution)/shard_map/all_to_all | solution.py:142
  176.8 15.3 %all-to-all-start = ((bf16[32,2,4096]{2,1,0:T(2,128)(2,1)}), bf16[32,2,4096]{2,1,0:T(2,128)(2,1)}, u32[]{:S(2)}, u32[]{:S(2)}) async-start(bf16[32,2,4096]{2,1,0:T(2,128)(2,1)} %reshape.350), calls=%async_computation | async-start | bytes 1048576 | tf_op jit(solution)/shard_map/all_to_all | solution.py:145
  197.6 3.6 copy-start.13
  239.1 4.1 copy-start.19
  249.2 4.1 copy-start.4
  253.3 5.2 %copy-start.25 = (f32[32,256,32]{1,2,0:T(8,128)S(1)}, f32[32,256,32]{1,2,0:T(8,128)}, u32[]{:S(2)}) copy-start(f32[32,256,32]{1,2,0:T(8,128)} %get-tuple-element.81) | copy-start | bytes 3145732
  253.3 5.2 %copy-start.26 = (f32[32,256,32]{1,2,0:T(8,128)S(1)}, f32[32,256,32]{1,2,0:T(8,128)}, u32[]{:S(2)}) copy-start(f32[32,256,32]{1,2,0:T(8,128)} %get-tuple-element.82) | copy-start | bytes 3145732
  253.3 5.2 %copy-start.27 = (f32[32,256,32]{1,2,0:T(8,128)S(1)}, f32[32,256,32]{1,2,0:T(8,128)}, u32[]{:S(2)}) copy-start(f32[32,256,32]{1,2,0:T(8,128)} %get-tuple-element.136) | copy-start | bytes 3145732
  253.3 5.3 %copy-start.28 = (f32[32,256,32]{1,2,0:T(8,128)S(1)}, f32[32,256,32]{1,2,0:T(8,128)}, u32[]{:S(2)}) copy-start(f32[32,256,32]{1,2,0:T(8,128)} %get-tuple-element.137) | copy-start | bytes 3145732
  276.7 3.4 copy-start
  280.0 3.4 copy-start.22
  283.4 3.2 copy-start.21
  363.2 6.4 %copy-start.30 = (f32[32,4096]{1,0:T(8,128)S(1)}, f32[32,4096]{1,0:T(8,128)}, u32[]{:S(2)}) copy-start(f32[32,4096]{1,0:T(8,128)} %div.87) | copy-start | bytes 1572868
  363.2 6.4 %copy-start.33 = (f32[64,4096]{1,0:T(8,128)S(1)}, f32[64,4096]{1,0:T(8,128)}, u32[]{:S(2)}) copy-start(f32[64,4096]{1,0:T(8,128)} %constant_dynamic-update-slice_fusion.1) | copy-start | bytes 3145732
  364.8 37.4 %all-to-all-start.6 = ((bf16[32,2,4096]{2,1,0:T(2,128)(2,1)}), bf16[32,2,4096]{2,1,0:T(2,128)(2,1)}, u32[]{:S(2)}, u32[]{:S(2)}) async-start(bf16[32,2,4096]{2,1,0:T(2,128)(2,1)} %reshape.362), calls=%async_computation.6 | async-start | bytes 1048576 | tf_op jit(solution)/shard_map/all_to_all | solution.py:162
  369.7 5.7 %copy-start.31 = (bf16[1,64,4096]{2,1,0:T(8,128)(2,1)S(1)}, bf16[1,64,4096]{2,1,0:T(8,128)(2,1)}, u32[]{:S(2)}) copy-start(bf16[1,64,4096]{2,1,0:T(8,128)(2,1)} %fusion.14) | copy-start | bytes 1572868
  400.6 11.5 %copy-start.14 = (bf16[1,32,64,128]{2,3,1,0:T(8,128)(2,1)S(1)}, bf16[1,32,64,128]{2,3,1,0:T(8,128)(2,1)}, u32[]{:S(2)}) copy-start(bf16[1,32,64,128]{2,3,1,0:T(8,128)(2,1)} %copy-done.13) | copy-start | bytes 1572868
  400.6 11.5 %copy-start.16 = (bf16[1,32,64,128]{2,3,1,0:T(8,128)(2,1)S(1)}, bf16[1,32,64,128]{2,3,1,0:T(8,128)(2,1)}, u32[]{:S(2)}) copy-start(bf16[1,32,64,128]{2,3,1,0:T(8,128)(2,1)} %copy-done.15) | copy-start | bytes 1572868
  402.2 10.7 %copy-start.29 = (bf16[1,64,4096]{2,1,0:T(8,128)(2,1)S(1)}, bf16[1,64,4096]{2,1,0:T(8,128)(2,1)}, u32[]{:S(2)}) copy-start(bf16[1,64,4096]{2,1,0:T(8,128)(2,1)} %get-tuple-element.85) | copy-start | bytes 1572868
  402.2 52.8 %all-to-all-start.5 = ((bf16[32,2,4096]{2,1,0:T(2,128)(2,1)}), bf16[32,2,4096]{2,1,0:T(2,128)(2,1)}, u32[]{:S(2)}, u32[]{:S(2)}) async-start(bf16[32,2,4096]{2,1,0:T(2,128)(2,1)} %reshape.360), calls=%async_computation.5 | async-start | bytes 1048576 | tf_op jit(solution)/shard_map/all_to_all | solution.py:161
  455.0 25.8 %all-to-all-start.4 = ((bf16[32,2,4096]{2,1,0:T(2,128)(2,1)}), bf16[32,2,4096]{2,1,0:T(2,128)(2,1)S(1)}, u32[]{:S(2)}, u32[]{:S(2)}) async-start(bf16[32,2,4096]{2,1,0:T(2,128)(2,1)} %reshape.358), calls=%async_computation.4 | async-start | bytes 1048576 | tf_op jit(solution)/shard_map/all_to_all | solution.py:160
  (12 other events, 22.8 us)
where the time goes:
time: 493 us; the launch traced here: 486 us
  other arithmetic  167 us (34%)
  local copies, waits for them, and re-layouts  149 us (30%)
  matrix products  76.3 us (15%)
  starting transfers between devices  57.3 us (12%)
  waiting for transfers between devices  19.4 us (4%)
  blocking collectives  14.1 us (3%)
    unnamed x7, other arithmetic  116 us
    unnamed x105, local copies, waits for them, and re-layouts  63.2 us
    concatenate x12, other arithmetic, negate_freq(): turned = jnp.roll(jnp.flip(spec, 1), 1, axis=1)  15.1 us
    psum x1, blocking collectives, body(): totals = lax.psum((partial_sums[0], partial_sums[1], partial_sums[2]), 'dp')  14.1 us
    div x4, local copies, waits for them, and re-layouts, inverse_dft(): out_im.reshape(channels, out_len) / padded_len  13.5 us
    rev x4, local copies, waits for them, and re-layouts, negate_freq(): flipped = jnp.flip(turned, 2)  12.1 us
    all_to_all x1, starting transfers between devices, body(): lax.all_to_all(key_proj, 'seq', split_axis=1, concat_axis=2, tiled=True)  11.7 us
    div x4, local copies, waits for them, and re-layouts, inverse_dft(): out_re.reshape(channels, out_len) / padded_len  11 us
  transfers between devices with their start and end apart: 7, of which 3 were waited for; matrix products, arithmetic and copies ran while one was open for 41% of the time, Pallas kernels for 0%

commit v1 on v0

v1 whole, which is shorter than its diff:
```python
import functools
import math

import jax
import jax.numpy as jnp
from jax import lax
from jax.experimental import pallas as pl
from jax.experimental.pallas import tpu as pltpu
from jax.sharding import PartitionSpec as P

F32 = jnp.float32
BF16 = jnp.bfloat16


def split(x):
    head = x.astype(BF16)
    return head, (x - head.astype(F32)).astype(BF16)


def stack_split(x):
    return jnp.concatenate(split(x), axis=0)


def mm(a, b):
    return lax.dot_general(a, b, (((1,), (0,)), ((), ())), preferred_element_type=F32)


def mm3(x, table):
    rows = table.shape[0] // 2
    head, rest = split(x)
    return mm(head, table[:rows]) + mm(rest, table[:rows]) + mm(head, table[rows:])


def twice(x):
    return jnp.concatenate([x, x], axis=1)


def tables_kernel(
    span, length, modes, dcol_ref, gcol_ref, drow_ref, tp_ref, tg_ref, wp_ref, wg_ref, cy_ref, cx_ref, q_ref
):
    group = tp_ref.shape[0]
    lane = lax.broadcasted_iota(jnp.int32, (span, span), 1)
    row = lax.broadcasted_iota(jnp.int32, (span, span), 0)
    up = lane.astype(F32) / length
    down = (span - lane).astype(F32) / length
    dcol = dcol_ref[...]
    gain = gcol_ref[...] / math.sqrt(length)
    tab_y = gain * jnp.exp(-dcol * up)
    tab_x = gain * jnp.exp(-dcol * down)
    cy_ref[0] = stack_split(tab_y)
    cx_ref[0] = stack_split(tab_x)
    for c in range(group):
        tap_y = jnp.sum(tab_y[c * modes : (c + 1) * modes], axis=0, keepdims=True)
        tap_x = jnp.sum(tab_x[c * modes : (c + 1) * modes], axis=0, keepdims=True)
        wide_y = jnp.broadcast_to(tap_y, (span, span))
        wide_x = jnp.broadcast_to(tap_x, (span, span))
        toe_y = pltpu.roll(wide_y, 0, 1, stride=1, stride_axis=0)
        toe_x = pltpu.roll(wide_x, 0, 1, stride=1, stride_axis=0)
        tp_ref[c] = stack_split(jnp.where(lane > row, toe_y, 0.0))
        tg_ref[c] = stack_split(jnp.where(lane < row, toe_x, 0.0))
    drow = drow_ref[0]
    down_r = (span - row).astype(F32) / length
    up_r = row.astype(F32) / length
    wp = jnp.exp(-drow * down_r)
    wg = jnp.exp(-drow * up_r)
    wp_ref[0, 0] = stack_split(wp)
    wp_ref[0, 1] = stack_split(wp * down_r)
    wg_ref[0, 0] = stack_split(wg)
    wg_ref[0, 1] = stack_split(wg * up_r)
    step = lax.broadcasted_iota(jnp.int32, (8, span), 0)
    power = lax.shift_left(jnp.ones_like(step), step).astype(F32) * (span / length)
    q_ref[0] = jnp.exp(-drow * power)


def gather_channels(src, scratch, group, chunks):
    scratch[...] = src.astype(F32).reshape(chunks * group, src.shape[-1])
    return [scratch[pl.ds(c, chunks, stride=group), :] for c in range(group)]


def channel_masks(group, modes, chunks, span):
    owner = lax.broadcasted_iota(jnp.int32, (chunks, span), 1) // modes
    return [owner == c for c in range(group)]


def keep_own(full, masks, chunks):
    out = jnp.zeros((chunks, full.shape[1]), F32)
    for c, mask in enumerate(masks):
        out = jnp.where(mask, full[c * chunks : (c + 1) * chunks], out)
    return out


def scan_forward(x, q):
    rows = x.shape[0]
    index = lax.broadcasted_iota(jnp.int32, x.shape, 0)
    for j in range(rows.bit_length() - 1):
        hop = 1 << j
        x = x + q[j : j + 1] * jnp.where(index >= hop, pltpu.roll(x, hop, 0), 0.0)
    return jnp.where(index >= 1, pltpu.roll(x, 1, 0), 0.0)


def scan_backward(x, q):
    rows = x.shape[0]
    index = lax.broadcasted_iota(jnp.int32, x.shape, 0)
    for j in range(rows.bit_length() - 1):
        hop = 1 << j
        x = x + q[j : j + 1] * jnp.where(index < rows - hop, pltpu.roll(x, rows - hop, 0), 0.0)
    return jnp.where(index < rows - 1, pltpu.roll(x, rows - 1, 0), 0.0)


def conv_kernel(
    modes, direct_ref, data_ref, tp_ref, tg_ref, wp_ref, wg_ref, cy_ref, cx_ref, q_ref,
    out_ref, state_ref, in_p, in_g, out_y, out_x
):
    chunks, _, group, span = data_ref.shape
    base = pl.program_id(0) * group
    prods = gather_channels(data_ref[:, 0], in_p, group, chunks)
    gmixs = gather_channels(data_ref[:, 1], in_g, group, chunks)
    prod_b = [twice(x.astype(BF16)) for x in prods]
    gmix_b = [twice(x.astype(BF16)) for x in gmixs]
    masks = channel_masks(group, modes, chunks, span)
    q = q_ref[0]
    left = keep_own(mm(jnp.concatenate(prod_b, axis=0), wp_ref[0, 0]), masks, chunks)
    right = keep_own(mm(jnp.concatenate(gmix_b, axis=0), wg_ref[0, 0]), masks, chunks)
    before = scan_forward(left, q)
    after = scan_backward(right, q)
    state_ref[0, 0] = before
    state_ref[0, 1] = right
    spread_y = jnp.concatenate([jnp.where(m, before, 0.0) for m in masks], axis=0)
    spread_x = jnp.concatenate([jnp.where(m, after, 0.0) for m in masks], axis=0)
    cross_y = mm3(spread_y, cy_ref[0])
    cross_x = mm3(spread_x, cx_ref[0])
    for c in range(group):
        direct = direct_ref[base + c]
        rows = slice(c * chunks, (c + 1) * chunks)
        y = mm(prod_b[c], tp_ref[c]) + cross_y[rows] + direct * prods[c]
        x = mm(gmix_b[c], tg_ref[c]) + cross_x[rows] + direct * gmixs[c]
        out_y[pl.ds(c, chunks, stride=group), :] = y
        out_x[pl.ds(c, chunks, stride=group), :] = x
    out_ref[:, 0] = out_y[...].reshape(chunks, group, span).astype(BF16)
    out_ref[:, 1] = out_x[...].reshape(chunks, group, span).astype(BF16)


def grads_kernel(modes, length, data_ref, state_ref, wp_ref, wg_ref, q_ref, out_ref, in_p, in_g):
    chunks, _, group, span = data_ref.shape
    prods = gather_channels(data_ref[:, 0], in_p, group, chunks)
    gmixs = gather_channels(data_ref[:, 1], in_g, group, chunks)
    prod_b = [x.astype(BF16) for x in prods]
    gmix_b = [x.astype(BF16) for x in gmixs]
    masks = channel_masks(group, modes, chunks, span)
    q = q_ref[0]
    before = state_ref[0, 0]
    right = state_ref[0, 1]
    aged = keep_own(mm(twice(jnp.concatenate(prod_b, axis=0)), wp_ref[0, 1]), masks, chunks)
    right_aged = keep_own(mm(twice(jnp.concatenate(gmix_b, axis=0)), wg_ref[0, 1]), masks, chunks)
    before_aged = scan_forward(aged + q[0:1] * before * (span / length), q)
    mode_sum = jnp.sum(right * before, axis=0, keepdims=True)
    rate_sum = jnp.sum(right_aged * before + right * before_aged, axis=0, keepdims=True)
    lane = lax.broadcasted_iota(jnp.int32, (span, span), 1)
    row = lax.broadcasted_iota(jnp.int32, (span, span), 0)
    mirror = jnp.where(lane + row == span - 1, 1.0, 0.0).astype(BF16)
    turned_b = mm(jnp.concatenate(prod_b, axis=0), mirror).astype(BF16)
    keep = lane <= row
    lag_rows = []
    for c in range(group):
        outer = lax.dot_general(
            turned_b[c * chunks : (c + 1) * chunks],
            gmix_b[c],
            (((0,), (0,)), ((), ())),
            preferred_element_type=F32,
        )
        turned = pltpu.roll(outer, 1, 1, stride=1, stride_axis=0)
        lag_rows.append(jnp.sum(jnp.where(keep, turned, 0.0), axis=0, keepdims=True))
    lags = jnp.concatenate(lag_rows, axis=0)
    owner = lax.broadcasted_iota(jnp.int32, (group, span), 1) // modes
    own = owner == lax.broadcasted_iota(jnp.int32, (group, span), 0)

    def pick(full):
        return jnp.sum(jnp.where(own, full, 0.0), axis=0, keepdims=True)

    mode_sum = mode_sum + pick(mm3(lags, wg_ref[0, 0]))
    rate_sum = rate_sum + pick(mm3(lags, wg_ref[0, 1]))
    skip_sum = pick(jnp.broadcast_to(lags[:, 0:1], lags.shape))
    out_ref[0, 0:1] = mode_sum
    out_ref[0, 1:2] = rate_sum
    out_ref[0, 2:3] = skip_sum
    out_ref[0, 3:8] = jnp.zeros((5, span), F32)


def whole_block(*shape):
    zeros = (0,) * (len(shape) - 1)
    return pl.BlockSpec(shape, lambda i: (i,) + zeros)


def build(parts, channels, span, modes, length):
    group = span // modes
    steps = channels // group
    double = 2 * span

    def tables(decay, gain):
        return pl.pallas_call(
            functools.partial(tables_kernel, span, length, modes),
            grid=(steps,),
            in_specs=[whole_block(span, 1), whole_block(span, 1), whole_block(1, 1, span)],
            out_specs=[
                whole_block(group, double, span),
                whole_block(group, double, span),
                whole_block(1, 2, double, span),
                whole_block(1, 2, double, span),
                whole_block(1, double, span),
                whole_block(1, double, span),
                whole_block(1, 8, span),
            ],
            out_shape=[
                jax.ShapeDtypeStruct((channels, double, span), BF16),
                jax.ShapeDtypeStruct((channels, double, span), BF16),
                jax.ShapeDtypeStruct((steps, 2, double, span), BF16),
                jax.ShapeDtypeStruct((steps, 2, double, span), BF16),
                jax.ShapeDtypeStruct((steps, double, span), BF16),
                jax.ShapeDtypeStruct((steps, double, span), BF16),
                jax.ShapeDtypeStruct((steps, 8, span), F32),
            ],
            name="tables",
        )(decay.reshape(steps * span, 1), gain.reshape(steps * span, 1), decay.reshape(steps, 1, span))

    data_spec = pl.BlockSpec((parts, 2, group, span), lambda i: (0, 0, i, 0))

    def conv(direct, data, tp, tg, wp, wg, cy, cx, q):
        return pl.pallas_call(
            functools.partial(conv_kernel, modes),
            grid=(steps,),
            in_specs=[
                pl.BlockSpec(memory_space=pltpu.SMEM),
                data_spec,
                whole_block(group, double, span),
                whole_block(group, double, span),
                whole_block(1, 1, double, span),
                whole_block(1, 1, double, span),
                whole_block(1, double, span),
                whole_block(1, double, span),
                whole_block(1, 8, span),
            ],
            out_specs=[data_spec, whole_block(1, 2, parts, span)],
            out_shape=[
                jax.ShapeDtypeStruct(data.shape, BF16),
                jax.ShapeDtypeStruct((steps, 2, parts, span), F32),
            ],
            scratch_shapes=[pltpu.VMEM((parts * group, span), F32)] * 4,
            name="conv",
        )(direct, data, tp, tg, wp, wg, cy, cx, q)

    def grads(data, states, wp, wg, q):
        return pl.pallas_call(
            functools.partial(grads_kernel, modes, length),
            grid=(steps,),
            in_specs=[
                data_spec,
                whole_block(1, 2, parts, span),
                whole_block(1, 2, double, span),
                whole_block(1, 2, double, span),
                whole_block(1, 8, span),
            ],
            out_specs=whole_block(1, 8, span),
            out_shape=jax.ShapeDtypeStruct((steps, 8, span), F32),
            scratch_shapes=[pltpu.VMEM((parts * group, span), F32)] * 2,
            name="grads",
        )(data, states, wp, wg, q)

    return tables, conv, grads


def times(a, b):
    return (a.astype(F32) * b.astype(F32)).astype(BF16)


def body(query_proj, key_proj, value_proj, grad_out, mode_gain, decay_rate, skip_gain):
    _, all_channels, span = query_proj.shape
    parts = lax.axis_size("seq")
    batch = lax.axis_size("dp")
    channels, modes = mode_gain.shape
    length = parts * span
    query, key, value, grad = query_proj[0], key_proj[0], value_proj[0], grad_out[0]
    product = times(key, value).reshape(parts, channels, span)
    grad_mix = times(grad, query).reshape(parts, channels, span)
    sent = jnp.stack([product, grad_mix], axis=1)
    data = lax.all_to_all(sent, "seq", split_axis=0, concat_axis=0, tiled=True)

    tables, conv, grads = build(parts, channels, span, modes, length)
    direct = skip_gain + jnp.sum(mode_gain, axis=1) / math.sqrt(length)
    tp, tg, wp, wg, cy, cx, q = tables(decay_rate, mode_gain)
    outs, states = conv(direct, data, tp, tg, wp, wg, cy, cx, q)
    back = lax.all_to_all(outs, "seq", split_axis=0, concat_axis=0, tiled=True)
    sums = lax.psum(grads(data, states, wp, wg, q), "dp")

    mixed = back[:, 0].reshape(all_channels, span)
    grad_prod = back[:, 1].reshape(all_channels, span)
    grad_query = times(grad, mixed)[None]
    grad_key = times(grad_prod, value)[None]
    grad_value = times(grad_prod, key)[None]
    scale = 1.0 / math.sqrt(batch * length)
    grad_modes = sums[:, 0].reshape(channels, modes) * (scale / math.sqrt(length))
    grad_rate = -mode_gain * sums[:, 1].reshape(channels, modes) * (scale / math.sqrt(length))
    grad_skip = sums[:, 2].reshape(channels, modes)[:, 0] * scale
    return (grad_query, grad_key, grad_value, grad_modes, grad_rate, grad_skip)


def solution(mesh):
    acts = P("dp", None, "seq")
    return jax.shard_map(
        body,
        mesh=mesh,
        in_specs=(acts, acts, acts, acts, P("seq", None), P("seq", None), P("seq")),
        out_specs=(acts, acts, acts, P("seq", None), P("seq", None), P("seq")),
        check_vma=False,
    )
```

time: 493 us -> 74.6 us (0.15); the launches traced: 486 us -> 73.4 us
  other arithmetic: 167 us -> 6.44 us
  local copies, waits for them, and re-layouts: 149 us -> 5.68 us
  matrix products: 76.3 us -> 0 us
  starting transfers between devices: 57.3 us -> 18.2 us
  Pallas kernels: 0 us -> 26.3 us
  waiting for transfers between devices: 19.4 us -> 4.85 us
    unnamed x7 -> x0, other arithmetic: 116 us -> none
    dot_general x32 -> x0, matrix products: 76.3 us -> none  [the longest x2 7.91 us: inverse_dft(): jnp.einsum('tk,ckj->ctj', sin_one, middle_re, precision=HIGHEST)]
    unnamed x105 -> x18, local copies, waits for them, and re-layouts: 63.2 us -> 2.52 us
    all_to_all x7 -> x2, starting transfers between devices: 57.3 us -> 18.2 us  [the longest x1 11.3 us: body(): data = lax.all_to_all(sent, 'seq', split_axis=0, concat_axis=0, tiled=True)]
    pallas_call x0 -> x3, Pallas kernels: none -> 26.3 us  [the longest x1 9.57 us: conv(): pl.pallas_call(functools.partial(conv_kernel, modes), grid=(steps,), in_s...]
    div x8 -> x0, local copies, waits for them, and re-layouts: 24.6 us -> none  [the longest x4 13.5 us: inverse_dft(): out_im.reshape(channels, out_len) / padded_len]
    slice x13 -> x1, local copies, waits for them, and re-layouts: 18.1 us -> 0.07 us  [body(): grad_prod = back[:, 1].reshape(all_channels, span)]
    convert_element_type x9 -> x0, local copies, waits for them, and re-layouts: 16.8 us -> none  [the longest x1 2.78 us: body(): key_grad = (grad_prod.astype(jnp.float32) * value_ch).astype(jnp.bfloat16)]
  transfers between devices with their start and end apart: 7 -> 2, of which waited for: 3 -> 1; matrix products, arithmetic and copies ran while one was open for 41% -> 8% of each run, Pallas kernels for 0% -> 23%
where the time goes in v1:
time: 74.6 us; the launch traced here: 73.4 us
  Pallas kernels  26.3 us (35%)
  starting transfers between devices  18.2 us (24%)
  blocking collectives  11.2 us (15%)
  other arithmetic  6.44 us (9%)
  local copies, waits for them, and re-layouts  5.68 us (8%)
  waiting for transfers between devices  4.85 us (7%)
  between operations  0.78 us (1%)
    all_to_all x1, starting transfers between devices, body(): data = lax.all_to_all(sent, 'seq', split_axis=0, concat_axis=0, tiled=True)  11.3 us
    psum x1, blocking collectives, body(): sums = lax.psum(grads(data, states, wp, wg, q), 'dp')  11.2 us
    pallas_call x1, Pallas kernels, conv(): pl.pallas_call(functools.partial(conv_kernel, modes), grid=(steps,), in_s...  9.57 us
    pallas_call x1, Pallas kernels, grads(): pl.pallas_call(functools.partial(grads_kernel, modes, length), grid=(step...  8.9 us
    pallas_call x1, Pallas kernels, tables(): pl.pallas_call(functools.partial(tables_kernel, span, length, modes), gri...  7.83 us
    all_to_all x1, starting transfers between devices, body(): back = lax.all_to_all(outs, 'seq', split_axis=0, concat_axis=0, tiled=True)  6.86 us
    all_to_all x1, waiting for transfers between devices, body(): data = lax.all_to_all(sent, 'seq', split_axis=0, concat_axis=0, tiled=True)  4.85 us
    convert_element_type x3, other arithmetic, times(): return (a.astype(F32) * b.astype(F32)).astype(BF16)  4.17 us
  transfers between devices with their start and end apart: 2, of which 1 were waited for; matrix products, arithmetic and copies ran while one was open for 8% of the time, Pallas kernels for 23%

profile of v1, /device:TPU:1, one launch (start us, length us, event | category | flops | bytes accessed | tf_op | source)
XLA Modules:
  0.0 73.4 jit_solution(16052393663386262813)
XLA Ops:
  0.6 0.0 copy-start.5
  0.6 0.0 copy-start.4
  0.7 1.3 %fusion = bf16[1,2048,128]{2,1,0:T(8,128)(2,1)S(1)} fusion(bf16[1,2048,128]{2,1,0:T(8,128)(2,1)} %param.10, bf16[1,2048,128]{2,1,0:T(8,128)(2,1)} %param.7), kind=kLoop, calls=%fused_computation.5 | loop fusion | flops 1048576 | bytes 1572864 | tf_op jit(solution)/shard_map/convert_element_type | solution.py:272
  2.0 0.0 copy-start.6
  2.0 1.3 %fusion.2 = bf16[1,2048,128]{2,1,0:T(8,128)(2,1)S(1)} fusion(bf16[1,2048,128]{2,1,0:T(8,128)(2,1)} %param.9, bf16[1,2048,128]{2,1,0:T(8,128)(2,1)} %param.8), kind=kLoop, calls=%fused_computation.7 | loop fusion | flops 1048576 | bytes 1572864 | tf_op jit(solution)/shard_map/convert_element_type | solution.py:272
  3.4 1.1 %pad_maximum_fusion = bf16[32,2,64,128]{3,2,1,0:T(8,128)(2,1)} fusion(bf16[32,1,64,128]{3,2,1,0:T(8,128)(2,1)S(1)} %bitcast.7, bf16[32,1,64,128]{3,2,1,0:T(8,128)(2,1)S(1)} %bitcast.8), kind=kLoop, calls=%fused_computation.10 | loop fusion | flops 524288 | bytes 2097152 | tf_op jit(solution)/shard_map/stack | solution.py:284
  4.4 11.3 %all-to-all-start = ((bf16[32,2,64,128]{3,2,1,0:T(8,128)(2,1)}), bf16[32,2,64,128]{3,2,1,0:T(8,128)(2,1)S(1)}, u32[]{:S(2)}, u32[]{:S(2)}) async-start(bf16[32,2,64,128]{3,2,1,0:T(8,128)(2,1)} %pad_maximum_fusion), calls=%async_computation | async-start | bytes 2097152 | tf_op jit(solution)/shard_map/all_to_all | solution.py:285
  15.8 0.1 copy.28
  15.9 0.7 reshape.112
  16.5 1.1 %reshape.115.dcol_ref = f32[1024,1]{1,0:T(8,128)} reshape(f32[64,16]{1,0:T(8,128)S(1)} %copy.28) | data formatting | bytes 8192 | tf_op jit(solution)/shard_map/reshape | solution.py:223
  17.6 0.1 copy.29
  17.7 1.1 %reshape.116.gcol_ref = f32[1024,1]{1,0:T(8,128)} reshape(f32[64,16]{1,0:T(8,128)S(1)} %copy.29) | data formatting | bytes 8192 | tf_op jit(solution)/shard_map/reshape | solution.py:223
  18.8 7.8 %tables.1 = (bf16[64,256,128]{2,1,0:T(8,128)(2,1)}, bf16[64,256,128]{2,1,0:T(8,128)(2,1)}, bf16[8,2,256,128]{3,2,1,0:T(8,128)(2,1)}, bf16[8,2,256,128]{3,2,1,0:T...) custom-call(f32[1024,1]{1,0:T(8,128)} %reshape.115.dcol_ref, ...), custom_call_target="tpu_custom_call" | custom-call | tf_op jit(solution)/shard_map/tables/pallas_call | solution.py:200
  26.7 0.5 multiply_add_fusion.direct_ref
  27.2 4.9 %all-to-all-done.data_ref = bf16[32,2,64,128]{3,2,1,0:T(8,128)(2,1)S(1)} async-done(((bf16[32,2,64,128]{3,2,1,0:T(8,128)(2,1)}), bf16[32,2,64,128]{3,2,1,0:T(8,128)(2,1)S(1)}, u32[]{:S(2)}, u32[]{:S(2)}) %all-to-all-start) | async-done | bytes 1048608 | tf_op jit(solution)/shard_map/all_to_all | solution.py:285
  32.1 1.0 %copy-done = bf16[32,2,64,128]{3,2,1,0:T(8,128)(2,1)} copy-done((bf16[32,2,64,128]{3,2,1,0:T(8,128)(2,1)}, bf16[32,2,64,128]{3,2,1,0:T(8,128)(2,1)S(1)}, u32[]{:S(2)}) %copy-start) | copy-done | bytes 1048600
  33.0 9.6 %conv.1 = (bf16[32,2,64,128]{3,2,1,0:T(8,128)(2,1)}, f32[8,2,32,128]{3,2,1,0:T(8,128)}) custom-call(f32[64]{0:T(128)} %multiply_add_fusion.direct_ref, bf16[32,2,64,128]{3,2,1,0:T(8,128)(2,1)} %copy-done, bf16[64,256,128]{2,1,0:T(8,128)(2,1)} %get-tuple-element.15.tp_ref, bf16[64,256,128]{2,1,0:T(8,128)(2,1)} %get-tuple-element.16.tg_ref, ...), custom_call_target="tpu_custom_call" | custom-call | tf_op jit(solution)/shard_map/conv/pallas_call | solution.py:228
  42.6 0.0 copy-start.1
  42.6 0.0 copy-start.2
  42.6 0.0 copy-start.3
  42.6 6.9 %all-to-all-start.1 = ((bf16[32,2,64,128]{3,2,1,0:T(8,128)(2,1)}), bf16[32,2,64,128]{3,2,1,0:T(8,128)(2,1)S(1)}, u32[]{:S(2)}, u32[]{:S(2)}) async-start(bf16[32,2,64,128]{3,2,1,0:T(8,128)(2,1)} %get-tuple-element.22), calls=%async_computation.1 | async-start | bytes 2097152 | tf_op jit(solution)/shard_map/all_to_all | solution.py:291
  49.5 8.9 %grads.1 = f32[8,8,128]{2,1,0:T(8,128)} custom-call(bf16[32,2,64,128]{3,2,1,0:T(8,128)(2,1)} %copy-done, f32[8,2,32,128]{3,2,1,0:T(8,128)} %get-tuple-element.23.state_ref, bf16[8,2,256,128]{3,2,1,0:T(8,128)(2,1)} %get-tuple-element.17.wp_ref, bf16[8,2,256,128]{3,2,1,0:T(8,128)(2,1)} %get-tuple-element.18.wg_ref, f32[8,8,128]{2,1,0:T(8,128)} %get-tuple-element.21.q_ref), custom_call_target="tpu_custom_call" | custom-call | tf_op jit(solution)/shard_map/grads/pallas_call | solution.py:252
  58.4 11.2 %psum.7 = f32[8,8,128]{2,1,0:T(8,128)S(1)} all-reduce(f32[8,8,128]{2,1,0:T(8,128)} %grads.1), channel_id=1, replica_groups=mesh['seq'=32,'dp'=4] {'dp'}, use_global_device_ids=true, to_apply=%region_1.0 | all-reduce | flops 8192 | bytes 65536 | tf_op jit(solution)/shard_map/psum | solution.py:292
  69.6 0.1 reshape_squeeze.10
  69.7 0.1 reshape_squeeze.4
  69.8 0.7 copy.36
  70.5 0.1 mul.61
  70.5 0.7 copy.35
  71.2 0.6 fusion.5
  71.8 0.0 all-to-all-done.1
  71.8 0.1 fusion.7
  71.9 1.5 %fusion.4 = (bf16[1,2048,128]{2,1,0:T(8,128)(2,1)}, bf16[1,2048,128]{2,1,0:T(8,128)(2,1)}, bf16[1,2048,128]{2,1,0:T(8,128)(2,1)}) fusion(bf16[1,2048,128]{2,1,0:T(8,128)(2,1)S(1)} %copy-done.1, bf16[1,2048,128]{2,1,0:T(8,128)(2,1)S(1)} %bitcast.9, bf16[1,2048,128]{2,1,0:T(8,128)(2,1)S(1)} %copy-done.3, bf16[1,2048,128]{2,1,0:T(8,128)(2,1)S(1)} %bitcast.10, ...), kind=kLoop, calls=%fused_computation.9 | loop fusion | flops 2883584 | bytes 4194304 | tf_op jit(solution)/shard_map/convert_element_type | solution.py:272
  (10 shorter events, 0.1 us)
Async XLA Ops:
  0.6 15.1 %copy-start.5 = (f32[64,16]{0,1:T(8,128)S(1)}, f32[64,16]{0,1:T(8,128)}, u32[]{:S(2)}) copy-start(f32[64,16]{0,1:T(8,128)} %param.12) | copy-start | bytes 12292
  0.6 17.0 %copy-start.4 = (f32[64,16]{0,1:T(8,128)S(1)}, f32[64,16]{0,1:T(8,128)}, u32[]{:S(2)}) copy-start(f32[64,16]{0,1:T(8,128)} %param.11) | copy-start | bytes 12292
  2.0 24.7 %copy-start.6 = (f32[64]{0:T(128)S(1)}, f32[64]{0:T(128)}, u32[]{:S(2)}) copy-start(f32[64]{0:T(128)} %param.13) | copy-start | bytes 772
  4.4 27.6 %all-to-all-start = ((bf16[32,2,64,128]{3,2,1,0:T(8,128)(2,1)}), bf16[32,2,64,128]{3,2,1,0:T(8,128)(2,1)S(1)}, u32[]{:S(2)}, u32[]{:S(2)}) async-start(bf16[32,2,64,128]{3,2,1,0:T(8,128)(2,1)} %pad_maximum_fusion), calls=%async_computation | async-start | bytes 2097152 | tf_op jit(solution)/shard_map/all_to_all | solution.py:285
  32.1 1.0 %copy-start = (bf16[32,2,64,128]{3,2,1,0:T(8,128)(2,1)}, bf16[32,2,64,128]{3,2,1,0:T(8,128)(2,1)S(1)}, u32[]{:S(2)}) copy-start(bf16[32,2,64,128]{3,2,1,0:T(8,128)(2,1)S(1)} %all-to-all-done.data_ref) | copy-start | bytes 3145732
  42.6 29.3 %copy-start.1 = (bf16[1,2048,128]{2,1,0:T(8,128)(2,1)S(1)}, bf16[1,2048,128]{2,1,0:T(8,128)(2,1)}, u32[]{:S(2)}) copy-start(bf16[1,2048,128]{2,1,0:T(8,128)(2,1)} %param.8) | copy-start | bytes 1572868
  42.6 29.3 %copy-start.2 = (bf16[1,2048,128]{2,1,0:T(8,128)(2,1)S(1)}, bf16[1,2048,128]{2,1,0:T(8,128)(2,1)}, u32[]{:S(2)}) copy-start(bf16[1,2048,128]{2,1,0:T(8,128)(2,1)} %param.10) | copy-start | bytes 1572868
  42.6 29.3 %copy-start.3 = (bf16[1,2048,128]{2,1,0:T(8,128)(2,1)S(1)}, bf16[1,2048,128]{2,1,0:T(8,128)(2,1)}, u32[]{:S(2)}) copy-start(bf16[1,2048,128]{2,1,0:T(8,128)(2,1)} %param.9) | copy-start | bytes 1572868
  42.6 29.2 %all-to-all-start.1 = ((bf16[32,2,64,128]{3,2,1,0:T(8,128)(2,1)}), bf16[32,2,64,128]{3,2,1,0:T(8,128)(2,1)S(1)}, u32[]{:S(2)}, u32[]{:S(2)}) async-start(bf16[32,2,64,128]{3,2,1,0:T(8,128)(2,1)} %get-tuple-element.22), calls=%async_computation.1 | async-start | bytes 2097152 | tf_op jit(solution)/shard_map/all_to_all | solution.py:291

commit v2 on v1

v2 whole, which is shorter than its diff:
```python
import functools
import math

import jax
import jax.numpy as jnp
from jax import lax
from jax.experimental import pallas as pl
from jax.experimental.pallas import tpu as pltpu
from jax.sharding import PartitionSpec as P

F32 = jnp.float32
BF16 = jnp.bfloat16


def split(x):
    head = x.astype(BF16)
    return head, (x - head.astype(F32)).astype(BF16)


def stack_split(x):
    return jnp.concatenate(split(x), axis=0)


def mm(a, b):
    return lax.dot_general(a, b, (((1,), (0,)), ((), ())), preferred_element_type=F32)


def mm3(x, table):
    rows = table.shape[0] // 2
    head, rest = split(x)
    return mm(head, table[:rows]) + mm(rest, table[:rows]) + mm(head, table[rows:])


def twice(x):
    return jnp.concatenate([x, x], axis=1)


def products_kernel(query_ref, key_ref, value_ref, grad_ref, out_ref):
    parts, _, channels, span = out_ref.shape

    def put(slot, a_ref, b_ref):
        out = a_ref[...].astype(F32) * b_ref[...].astype(F32)
        out_ref[:, slot] = out.astype(BF16).reshape(parts, channels, span)

    put(0, key_ref, value_ref)
    put(1, grad_ref, query_ref)


def tables_kernel(length, decay_ref, gain_ref, tp_ref, tg_ref, wp_ref, wg_ref, cy_ref, cx_ref, q_ref):
    modes, channels = decay_ref.shape
    per = cy_ref.shape[0]
    span = cy_ref.shape[2]
    group = span // modes
    lane = lax.broadcasted_iota(jnp.int32, (span, span), 1)
    row = lax.broadcasted_iota(jnp.int32, (span, span), 0)
    up = lane.astype(F32) / length
    down = (span - lane).astype(F32) / length
    up_r = row.astype(F32) / length
    down_r = (span - row).astype(F32) / length
    step = lax.broadcasted_iota(jnp.int32, (8, span), 0)
    power = lax.shift_left(jnp.ones_like(step), step).astype(F32) * (span / length)
    first = pl.program_id(0) * (per * group)
    pad = jnp.zeros((modes, span - channels), F32)

    def turned(ref):
        return pltpu.roll(jnp.concatenate([ref[...], pad], axis=1), span - first, 1)

    decay = turned(decay_ref)
    gain = turned(gain_ref) / math.sqrt(length)
    for u in range(per):
        picks = range(u * group, (u + 1) * group)
        dcol = jnp.concatenate([jnp.broadcast_to(decay[:, c : c + 1], (modes, span)) for c in picks], axis=0)
        gcol = jnp.concatenate([jnp.broadcast_to(gain[:, c : c + 1], (modes, span)) for c in picks], axis=0)
        tab_y = gcol * jnp.exp(-dcol * up)
        tab_x = gcol * jnp.exp(-dcol * down)
        cy_ref[u] = stack_split(tab_y)
        cx_ref[u] = stack_split(tab_x)
        for c in range(group):
            tap_y = jnp.sum(tab_y[c * modes : (c + 1) * modes], axis=0, keepdims=True)
            tap_x = jnp.sum(tab_x[c * modes : (c + 1) * modes], axis=0, keepdims=True)
            wide_y = jnp.broadcast_to(tap_y, (span, span))
            wide_x = jnp.broadcast_to(tap_x, (span, span))
            toe_y = pltpu.roll(wide_y, 0, 1, stride=1, stride_axis=0)
            toe_x = pltpu.roll(wide_x, 0, 1, stride=1, stride_axis=0)
            tp_ref[u * group + c] = stack_split(jnp.where(lane > row, toe_y, 0.0))
            tg_ref[u * group + c] = stack_split(jnp.where(lane < row, toe_x, 0.0))
        drow = jnp.sum(jnp.where(lane == row, dcol, 0.0), axis=0, keepdims=True)
        wp = jnp.exp(-drow * down_r)
        wg = jnp.exp(-drow * up_r)
        wp_ref[u, 0] = stack_split(wp)
        wp_ref[u, 1] = stack_split(wp * down_r)
        wg_ref[u, 0] = stack_split(wg)
        wg_ref[u, 1] = stack_split(wg * up_r)
        q_ref[u] = jnp.exp(-drow * power)


def gather_channels(data_ref, slot, first, scratch, group):
    chunks, _, _, span = data_ref.shape
    picked = data_ref[:, slot, pl.ds(pl.multiple_of(first, group), group), :]
    scratch[...] = picked.astype(F32).reshape(chunks * group, span)
    return [scratch[pl.ds(c, chunks, stride=group), :] for c in range(group)]


def channel_masks(group, modes, chunks, span):
    owner = lax.broadcasted_iota(jnp.int32, (chunks, span), 1) // modes
    return [owner == c for c in range(group)]


def keep_own(full, masks, chunks):
    out = jnp.zeros((chunks, full.shape[1]), F32)
    for c, mask in enumerate(masks):
        out = jnp.where(mask, full[c * chunks : (c + 1) * chunks], out)
    return out


def scan_forward(x, q):
    rows = x.shape[0]
    index = lax.broadcasted_iota(jnp.int32, x.shape, 0)
    for j in range(rows.bit_length() - 1):
        hop = 1 << j
        x = x + q[j : j + 1] * jnp.where(index >= hop, pltpu.roll(x, hop, 0), 0.0)
    return jnp.where(index >= 1, pltpu.roll(x, 1, 0), 0.0)


def scan_backward(x, q):
    rows = x.shape[0]
    index = lax.broadcasted_iota(jnp.int32, x.shape, 0)
    for j in range(rows.bit_length() - 1):
        hop = 1 << j
        x = x + q[j : j + 1] * jnp.where(index < rows - hop, pltpu.roll(x, rows - hop, 0), 0.0)
    return jnp.where(index < rows - 1, pltpu.roll(x, rows - 1, 0), 0.0)


def conv_kernel(
    modes, direct_ref, data_ref, tp_ref, tg_ref, wp_ref, wg_ref, cy_ref, cx_ref, q_ref,
    out_ref, state_ref, in_p, in_g, out_y, out_x
):
    chunks, _, _, span = data_ref.shape
    per = q_ref.shape[0]
    group = span // modes
    base = pl.program_id(0) * (per * group)
    masks = channel_masks(group, modes, chunks, span)
    for u in range(per):
        first = base + u * group
        prods = gather_channels(data_ref, 0, first, in_p.at[u], group)
        gmixs = gather_channels(data_ref, 1, first, in_g.at[u], group)
        prod_b = [twice(x.astype(BF16)) for x in prods]
        gmix_b = [twice(x.astype(BF16)) for x in gmixs]
        q = q_ref[u]
        left = keep_own(mm(jnp.concatenate(prod_b, axis=0), wp_ref[u, 0]), masks, chunks)
        right = keep_own(mm(jnp.concatenate(gmix_b, axis=0), wg_ref[u, 0]), masks, chunks)
        before = scan_forward(left, q)
        after = scan_backward(right, q)
        state_ref[u, 0] = before
        state_ref[u, 1] = right
        spread_y = jnp.concatenate([jnp.where(m, before, 0.0) for m in masks], axis=0)
        spread_x = jnp.concatenate([jnp.where(m, after, 0.0) for m in masks], axis=0)
        cross_y = mm3(spread_y, cy_ref[u])
        cross_x = mm3(spread_x, cx_ref[u])
        for c in range(group):
            direct = direct_ref[first + c]
            rows = slice(c * chunks, (c + 1) * chunks)
            k = u * group + c
            y = mm(prod_b[c], tp_ref[k]) + cross_y[rows] + direct * prods[c]
            x = mm(gmix_b[c], tg_ref[k]) + cross_x[rows] + direct * gmixs[c]
            out_y[u, pl.ds(c, chunks, stride=group), :] = y
            out_x[u, pl.ds(c, chunks, stride=group), :] = x
        place = slice(u * group, (u + 1) * group)
        out_ref[:, 0, place] = out_y[u].reshape(chunks, group, span).astype(BF16)
        out_ref[:, 1, place] = out_x[u].reshape(chunks, group, span).astype(BF16)


def grads_kernel(modes, length, data_ref, state_ref, wp_ref, wg_ref, q_ref, out_ref, in_p, in_g, rows_ref):
    chunks, _, channels, span = data_ref.shape
    per = q_ref.shape[0]
    group = span // modes
    base = pl.program_id(0) * (per * group)
    masks = channel_masks(group, modes, chunks, span)
    lane = lax.broadcasted_iota(jnp.int32, (span, span), 1)
    row = lax.broadcasted_iota(jnp.int32, (span, span), 0)
    mirror = jnp.where(lane + row == span - 1, 1.0, 0.0).astype(BF16)
    keep = lane <= row
    owner = lax.broadcasted_iota(jnp.int32, (group, span), 1) // modes
    own = owner == lax.broadcasted_iota(jnp.int32, (group, span), 0)
    for u in range(per):
        first = base + u * group
        prods = gather_channels(data_ref, 0, first, in_p.at[u], group)
        gmixs = gather_channels(data_ref, 1, first, in_g.at[u], group)
        prod_b = jnp.concatenate([x.astype(BF16) for x in prods], axis=0)
        gmix_b = jnp.concatenate([x.astype(BF16) for x in gmixs], axis=0)
        q = q_ref[u]
        before = state_ref[u, 0]
        right = state_ref[u, 1]
        aged = keep_own(mm(twice(prod_b), wp_ref[u, 1]), masks, chunks)
        right_aged = keep_own(mm(twice(gmix_b), wg_ref[u, 1]), masks, chunks)
        before_aged = scan_forward(aged + q[0:1] * before * (span / length), q)
        mode_sum = jnp.sum(right * before, axis=0, keepdims=True)
        rate_sum = jnp.sum(right_aged * before + right * before_aged, axis=0, keepdims=True)
        turned_b = mm(prod_b, mirror).astype(BF16)
        lag_rows = []
        for c in range(group):
            rows = slice(c * chunks, (c + 1) * chunks)
            outer = lax.dot_general(
                turned_b[rows], gmix_b[rows], (((0,), (0,)), ((), ())), preferred_element_type=F32
            )
            turned = pltpu.roll(outer, 1, 1, stride=1, stride_axis=0)
            lag_rows.append(jnp.sum(jnp.where(keep, turned, 0.0), axis=0, keepdims=True))
        lags = jnp.concatenate(lag_rows, axis=0)
        place = pl.ds(pl.multiple_of(first, group), group)
        rows_ref[0, place, :] = jnp.where(own, mm3(lags, wg_ref[u, 0]) + mode_sum, 0.0)
        rows_ref[1, place, :] = jnp.where(own, mm3(lags, wg_ref[u, 1]) + rate_sum, 0.0)
        rows_ref[2, place, :] = jnp.where(own, lags[:, 0:1], 0.0)

    @pl.when(pl.program_id(0) == pl.num_programs(0) - 1)
    def _():
        mode = lax.broadcasted_iota(jnp.int32, (modes, span), 0)
        at = lax.broadcasted_iota(jnp.int32, (modes, span), 1)
        choose = jnp.where(lax.rem(at, modes) == mode, 1.0, 0.0)
        for k in range(3):
            out_ref[k] = lax.dot_general(
                choose,
                rows_ref[k],
                (((1,), (1,)), ((), ())),
                precision=lax.Precision.HIGHEST,
                preferred_element_type=F32,
            )


def whole_block(*shape):
    zeros = (0,) * (len(shape) - 1)
    return pl.BlockSpec(shape, lambda i: (i,) + zeros)


def build(parts, all_channels, channels, span, modes, length, per):
    group = span // modes
    steps = channels // group
    double = 2 * span
    whole = pl.BlockSpec(memory_space=pltpu.VMEM)

    def products(query, key, value, grad, cuts=4):
        rows = pl.BlockSpec((all_channels // cuts, span), lambda i: (i, 0))
        return pl.pallas_call(
            products_kernel,
            grid=(cuts,),
            in_specs=[rows] * 4,
            out_specs=whole_block(parts // cuts, 2, channels, span),
            out_shape=jax.ShapeDtypeStruct((parts, 2, channels, span), BF16),
            name="products",
        )(query, key, value, grad)

    def tables(decay, gain):
        return pl.pallas_call(
            functools.partial(tables_kernel, length),
            grid=(steps // per,),
            in_specs=[whole, whole],
            out_specs=[
                whole_block(per * group, double, span),
                whole_block(per * group, double, span),
                whole_block(per, 2, double, span),
                whole_block(per, 2, double, span),
                whole_block(per, double, span),
                whole_block(per, double, span),
                whole_block(per, 8, span),
            ],
            out_shape=[
                jax.ShapeDtypeStruct((channels, double, span), BF16),
                jax.ShapeDtypeStruct((channels, double, span), BF16),
                jax.ShapeDtypeStruct((steps, 2, double, span), BF16),
                jax.ShapeDtypeStruct((steps, 2, double, span), BF16),
                jax.ShapeDtypeStruct((steps, double, span), BF16),
                jax.ShapeDtypeStruct((steps, double, span), BF16),
                jax.ShapeDtypeStruct((steps, 8, span), F32),
            ],
            name="tables",
        )(decay, gain)

    def conv(direct, data, tp, tg, wp, wg, cy, cx, q):
        return pl.pallas_call(
            functools.partial(conv_kernel, modes),
            grid=(steps // per,),
            in_specs=[
                pl.BlockSpec(memory_space=pltpu.SMEM),
                whole,
                whole_block(per * group, double, span),
                whole_block(per * group, double, span),
                whole_block(per, 1, double, span),
                whole_block(per, 1, double, span),
                whole_block(per, double, span),
                whole_block(per, double, span),
                whole_block(per, 8, span),
            ],
            out_specs=[
                pl.BlockSpec((parts, 2, per * group, span), lambda i: (0, 0, i, 0)),
                whole_block(per, 2, parts, span),
            ],
            out_shape=[
                jax.ShapeDtypeStruct(data.shape, BF16),
                jax.ShapeDtypeStruct((steps, 2, parts, span), F32),
            ],
            scratch_shapes=[pltpu.VMEM((per, parts * group, span), F32)] * 4,
            name="conv",
        )(direct, data, tp, tg, wp, wg, cy, cx, q)

    def grads(data, states, wp, wg, q):
        return pl.pallas_call(
            functools.partial(grads_kernel, modes, length),
            grid=(steps // per,),
            in_specs=[
                whole,
                whole_block(per, 2, parts, span),
                whole_block(per, 2, double, span),
                whole_block(per, 2, double, span),
                whole_block(per, 8, span),
            ],
            out_specs=whole,
            out_shape=jax.ShapeDtypeStruct((3, modes, channels), F32),
            scratch_shapes=[pltpu.VMEM((per, parts * group, span), F32)] * 2
            + [pltpu.VMEM((3, channels, span), F32)],
            name="grads",
        )(data, states, wp, wg, q)

    return products, tables, conv, grads


def times(a, b):
    return (a.astype(F32) * b.astype(F32)).astype(BF16)


def exchange(x):
    return lax.all_to_all(x, "seq", split_axis=0, concat_axis=0, tiled=True)


def butterfly_sum(x, axis):
    size = lax.axis_size(axis)
    hop = 1
    while hop < size:
        x = x + lax.ppermute(x, axis, [(i, i ^ hop) for i in range(size)])
        hop *= 2
    return x


def body(query_proj, key_proj, value_proj, grad_out, mode_gain, decay_rate, skip_gain):
    _, all_channels, span = query_proj.shape
    parts = lax.axis_size("seq")
    batch = lax.axis_size("dp")
    channels, modes = mode_gain.shape
    length = parts * span
    query, key, value, grad = query_proj[0], key_proj[0], value_proj[0], grad_out[0]
    products, tables, conv, grads = build(parts, all_channels, channels, span, modes, length, 2)
    sent = products(query, key, value, grad)
    data = pltpu.with_memory_space_constraint(exchange(sent), pltpu.VMEM)

    direct = skip_gain + jnp.sum(mode_gain, axis=1) / math.sqrt(length)
    tp, tg, wp, wg, cy, cx, q = tables(decay_rate.T, mode_gain.T)
    outs, states = conv(direct, data, tp, tg, wp, wg, cy, cx, q)
    back = exchange(outs)
    sums = butterfly_sum(grads(data, states, wp, wg, q), "dp")

    mixed = back[:, 0].reshape(all_channels, span)
    grad_prod = back[:, 1].reshape(all_channels, span)
    grad_query = times(grad, mixed)[None]
    grad_key = times(grad_prod, value)[None]
    grad_value = times(grad_prod, key)[None]
    scale = 1.0 / math.sqrt(batch * length)
    grad_modes = (sums[0] * (scale / math.sqrt(length))).T
    grad_rate = (-mode_gain.T * sums[1] * (scale / math.sqrt(length))).T
    grad_skip = sums[2, 0] * scale
    return (grad_query, grad_key, grad_value, grad_modes, grad_rate, grad_skip)


def solution(mesh):
    acts = P("dp", None, "seq")
    return jax.shard_map(
        body,
        mesh=mesh,
        in_specs=(acts, acts, acts, acts, P("seq", None), P("seq", None), P("seq")),
        out_specs=(acts, acts, acts, P("seq", None), P("seq", None), P("seq")),
        check_vma=False,
    )
```

time: 74.6 us -> 67.6 us (0.906)
  the two profiles are of different devices: /device:TPU:1 before, /device:TPU:0 now
where the time goes in v2:
time: 67.6 us; the launch traced here: 66.9 us
  Pallas kernels  26.1 us (39%)
  waiting for transfers between devices  17.7 us (26%)
  starting transfers between devices  16.8 us (25%)
  other arithmetic  5.5 us (8%)
  between operations  0.74 us (1%)
    all_to_all x2, starting transfers between devices, exchange(): return lax.all_to_all(x, 'seq', split_axis=0, concat_axis=0, tiled=True)  16.2 us
    all_to_all x2, waiting for transfers between devices, exchange(): return lax.all_to_all(x, 'seq', split_axis=0, concat_axis=0, tiled=True)  13.1 us
    pallas_call x1, Pallas kernels, grads(): pl.pallas_call(functools.partial(grads_kernel, modes, length), grid=(step...  7.91 us
    pallas_call x1, Pallas kernels, conv(): pl.pallas_call(functools.partial(conv_kernel, modes), grid=(steps // per,...  7.89 us
    pallas_call x1, Pallas kernels, tables(): pl.pallas_call(functools.partial(tables_kernel, length), grid=(steps // p...  6.55 us
    ppermute x2, waiting for transfers between devices, butterfly_sum(): x = x + lax.ppermute(x, axis, [(i, i ^ hop) for i in range(size)])  4.64 us
    pallas_call x1, Pallas kernels, products(): pl.pallas_call(products_kernel, grid=(cuts,), in_specs=[rows] * 4, out_sp...  3.72 us
    convert_element_type x1, other arithmetic, times(): return (a.astype(F32) * b.astype(F32)).astype(BF16)  2.5 us
  transfers between devices with their start and end apart: 4, of which 4 were waited for; matrix products, arithmetic and copies ran while one was open for 4% of the time, Pallas kernels for 22%

profile of v2, /device:TPU:0, one launch (start us, length us, event | category | flops | bytes accessed | tf_op | source)
XLA Modules:
  0.0 66.9 jit_solution(8607775437017128280)
XLA Ops:
  0.6 0.0 copy-start.2
  0.6 0.0 copy-start.4
  0.7 3.7 %products.1 = bf16[32,2,64,128]{3,2,1,0:T(8,128)(2,1)} custom-call(bf16[2048,128]{1,0:T(8,128)(2,1)} %bitcast.32, bf16[2048,128]{1,0:T(8,128)(2,1)} %bitcast.27, bf16[2048,128]{1,0:T(8,128)(2,1)} %bitcast.28, bf16[2048,128]{1,0:T(8,128)(2,1)} %bitcast.29), custom_call_target="tpu_custom_call" | custom-call | tf_op jit(solution)/shard_map/products/pallas_call | solution.py:242
  4.4 10.9 %all-to-all-start = ((bf16[32,2,64,128]{3,2,1,0:T(8,128)(2,1)}), bf16[32,2,64,128]{3,2,1,0:T(8,128)(2,1)S(1)}, u32[]{:S(2)}, u32[]{:S(2)}) async-start(bf16[32,2,64,128]{3,2,1,0:T(8,128)(2,1)} %products.1), calls=%async_computation | async-start | bytes 2097152 | tf_op jit(solution)/shard_map/all_to_all | solution.py:330
  15.3 0.0 copy-done.2
  15.3 6.6 %tables.1 = (bf16[64,256,128]{2,1,0:T(8,128)(2,1)}, bf16[64,256,128]{2,1,0:T(8,128)(2,1)}, bf16[8,2,256,128]{3,2,1,0:T(8,128)(2,1)}, bf16[8,2,256,128]{3,2,1,0:T...) custom-call(f32[16,64]{1,0:T(8,128)} %bitcast.34, f32[16,64]{1,0:T(8,128)} %bitcast.33), custom_call_target="tpu_custom_call" | custom-call | tf_op jit(solution)/shard_map/tables/pallas_call | solution.py:252
  21.9 0.0 copy-done.4
  21.9 0.5 multiply_add_fusion.direct_ref
  22.4 10.8 %all-to-all-done.data_ref = bf16[32,2,64,128]{3,2,1,0:T(8,128)(2,1)S(1)} async-done(((bf16[32,2,64,128]{3,2,1,0:T(8,128)(2,1)}), bf16[32,2,64,128]{3,2,1,0:T(8,128)(2,1)S(1)}, u32[]{:S(2)}, u32[]{:S(2)}) %all-to-all-start) | async-done | bytes 1048608 | tf_op jit(solution)/shard_map/all_to_all | solution.py:330
  33.2 7.9 %conv.1 = (bf16[32,2,64,128]{3,2,1,0:T(8,128)(2,1)}, f32[8,2,32,128]{3,2,1,0:T(8,128)}) custom-call(f32[64]{0:T(128)} %multiply_add_fusion.direct_ref, bf16[32,2,64,128]{3,2,1,0:T(8,128)(2,1)S(1)} %all-to-all-done.data_ref, bf16[64,256,128]{2,1,0:T(8,128)(2,1)} %get-tuple-element.15.tp_ref, bf16[64,256,128]{2,1,0:T(8,128)(2,1)} %get-tuple-element.16.tg_ref, ...), custom_call_target="tpu_custom_call" | custom-call | tf_op jit(solution)/shard_map/conv/pallas_call | solution.py:278
  41.1 0.0 copy-start.3
  41.1 0.0 copy-start
  41.1 0.0 copy-start.1
  41.1 5.3 %all-to-all-start.1 = ((bf16[32,2,64,128]{3,2,1,0:T(8,128)(2,1)}), bf16[32,2,64,128]{3,2,1,0:T(8,128)(2,1)S(1)}, u32[]{:S(2)}, u32[]{:S(2)}) async-start(bf16[32,2,64,128]{3,2,1,0:T(8,128)(2,1)} %get-tuple-element.22), calls=%async_computation.1 | async-start | bytes 2097152 | tf_op jit(solution)/shard_map/all_to_all | solution.py:330
  46.5 7.9 %grads.1 = f32[3,16,64]{2,1,0:T(8,128)} custom-call(bf16[32,2,64,128]{3,2,1,0:T(8,128)(2,1)S(1)} %all-to-all-done.data_ref, f32[8,2,32,128]{3,2,1,0:T(8,128)} %get-tuple-element.23.state_ref, bf16[8,2,256,128]{3,2,1,0:T(8,128)(2,1)} %get-tuple-element.17.wp_ref, bf16[8,2,256,128]{3,2,1,0:T(8,128)(2,1)} %get-tuple-element.18.wg_ref, ...), custom_call_target="tpu_custom_call" | custom-call | tf_op jit(solution)/shard_map/grads/pallas_call | solution.py:305
  54.4 0.0 collective-permute-start
  54.4 1.4 %collective-permute-done = f32[3,16,64]{2,1,0:T(8,128)S(1)} collective-permute-done((f32[3,16,64]{2,1,0:T(8,128)}, f32[3,16,64]{2,1,0:T(8,128)S(1)}, u32[]{:S(2)}, u32[]{:S(2)}) %collective-permute-start) | collective-permute-done | bytes 12320 | tf_op jit(solution)/shard_map/ppermute | solution.py:337
  55.8 0.7 %add.10 = f32[3,16,64]{2,1,0:T(8,128)S(1)} add(f32[3,16,64]{2,1,0:T(8,128)} %grads.1, f32[3,16,64]{2,1,0:T(8,128)S(1)} %collective-permute-done) | non-fusion elementwise | flops 3072 | bytes 36864 | tf_op jit(solution)/shard_map/add | solution.py:337
  56.5 0.6 collective-permute-start.1
  57.1 3.2 %collective-permute-done.1 = f32[3,16,64]{2,1,0:T(8,128)S(1)} collective-permute-done((f32[3,16,64]{2,1,0:T(8,128)S(1)}, f32[3,16,64]{2,1,0:T(8,128)S(1)}, u32[]{:S(2)}, u32[]{:S(2)}) %collective-permute-start.1) | collective-permute-done | bytes 12320 | tf_op jit(solution)/shard_map/ppermute | solution.py:337
  60.4 0.5 fusion.7
  60.9 0.6 fusion.6
  61.5 0.0 copy-done.3
  61.5 0.6 fusion.5
  62.1 2.3 %all-to-all-done.1 = bf16[32,2,64,128]{3,2,1,0:T(8,128)(2,1)S(1)} async-done(((bf16[32,2,64,128]{3,2,1,0:T(8,128)(2,1)}), bf16[32,2,64,128]{3,2,1,0:T(8,128)(2,1)S(1)}, u32[]{:S(2)}, u32[]{:S(2)}) %all-to-all-start.1) | async-done | bytes 1048608 | tf_op jit(solution)/shard_map/all_to_all | solution.py:330
  64.3 0.1 fusion.8
  64.4 0.0 copy-done
  64.4 0.0 copy-done.1
  64.4 2.5 %fusion.1 = (bf16[1,2048,128]{2,1,0:T(8,128)(2,1)}, bf16[1,2048,128]{2,1,0:T(8,128)(2,1)}, bf16[1,2048,128]{2,1,0:T(8,128)(2,1)}) fusion(bf16[1,2048,128]{2,1,0:T(8,128)(2,1)S(1)} %bitcast.30, bf16[1,2048,128]{2,1,0:T(8,128)(2,1)S(1)} %copy-done, bf16[1,2048,128]{2,1,0:T(8,128)(2,1)S(1)} %copy-done.1, bf16[1,2048,128]{2,1,0:T(8,128)(2,1)S(1)} %bitcast.31, ...), kind=kLoop, calls=%fused_computation.3 | loop fusion | flops 2883584 | bytes 4194304 | tf_op jit(solution)/shard_map/convert_element_type | solution.py:326
  (2 shorter events, 0.0 us)
Async XLA Ops:
  0.6 14.7 %copy-start.2 = (f32[64,16]{0,1:T(8,128)S(1)}, f32[64,16]{0,1:T(8,128)}, u32[]{:S(2)}) copy-start(f32[64,16]{0,1:T(8,128)} %param.11) | copy-start | bytes 12292
  0.6 21.2 %copy-start.4 = (f32[64]{0:T(128)S(1)}, f32[64]{0:T(128)}, u32[]{:S(2)}) copy-start(f32[64]{0:T(128)} %param.13) | copy-start | bytes 772
  4.4 28.8 %all-to-all-start = ((bf16[32,2,64,128]{3,2,1,0:T(8,128)(2,1)}), bf16[32,2,64,128]{3,2,1,0:T(8,128)(2,1)S(1)}, u32[]{:S(2)}, u32[]{:S(2)}) async-start(bf16[32,2,64,128]{3,2,1,0:T(8,128)(2,1)} %products.1), calls=%async_computation | async-start | bytes 2097152 | tf_op jit(solution)/shard_map/all_to_all | solution.py:330
  41.1 20.4 %copy-start.3 = (f32[64,16]{0,1:T(8,128)S(1)}, f32[64,16]{0,1:T(8,128)}, u32[]{:S(2)}) copy-start(f32[64,16]{0,1:T(8,128)} %param.11) | copy-start | bytes 12292
  41.1 23.3 %copy-start = (bf16[1,2048,128]{2,1,0:T(8,128)(2,1)S(1)}, bf16[1,2048,128]{2,1,0:T(8,128)(2,1)}, u32[]{:S(2)}) copy-start(bf16[1,2048,128]{2,1,0:T(8,128)(2,1)} %param.8) | copy-start | bytes 1572868
  41.1 23.3 %copy-start.1 = (bf16[1,2048,128]{2,1,0:T(8,128)(2,1)S(1)}, bf16[1,2048,128]{2,1,0:T(8,128)(2,1)}, u32[]{:S(2)}) copy-start(bf16[1,2048,128]{2,1,0:T(8,128)(2,1)} %param.9) | copy-start | bytes 1572868
  41.1 23.2 %all-to-all-start.1 = ((bf16[32,2,64,128]{3,2,1,0:T(8,128)(2,1)}), bf16[32,2,64,128]{3,2,1,0:T(8,128)(2,1)S(1)}, u32[]{:S(2)}, u32[]{:S(2)}) async-start(bf16[32,2,64,128]{3,2,1,0:T(8,128)(2,1)} %get-tuple-element.22), calls=%async_computation.1 | async-start | bytes 2097152 | tf_op jit(solution)/shard_map/all_to_all | solution.py:330
  54.4 1.4 %collective-permute-start = (f32[3,16,64]{2,1,0:T(8,128)}, f32[3,16,64]{2,1,0:T(8,128)S(1)}, u32[]{:S(2)}, u32[]{:S(2)}) collective-permute-start(f32[3,16,64]{2,1,0:T(8,128)} %grads.1), channel_id=1, source_target_pairs={{0,1},{1,0},{2,3},{3,2},{4,5},{5,4},{6,7},{7,6},{8,9},{9,8},{10,11... | collective-permute-start | bytes 36872 | tf_op jit(solution)/shard_map/ppermute | solution.py:337
  56.5 3.8 %collective-permute-start.1 = (f32[3,16,64]{2,1,0:T(8,128)S(1)}, f32[3,16,64]{2,1,0:T(8,128)S(1)}, u32[]{:S(2)}, u32[]{:S(2)}) collective-permute-start(f32[3,16,64]{2,1,0:T(8,128)S(1)} %add.10), channel_id=1, source_target_pairs={{0,2},{1,3},{2,0},{3,1},{4,6},{5,7},{6,4},{7,5},{8,10},{9,11},{10,... | collective-permute-start | bytes 36872 | tf_op jit(solution)/shard_map/ppermute | solution.py:337
